TPU v7x, 128 devices: a whole 4x4x4 slice. The times are simulated.
128 devices in a mesh: dp: 16 (over z_hi, x, core), tensor: 8 (over z_lo, y).
Axes of the slice: x: 4, y: 4, z: 4 (z_hi: 2, z_lo: 2; z = z_hi * 2 + z_lo), core: 2. Of those that a mesh axis runs over, the one named last changes fastest.
Arguments:
- tokens: bfloat16 [16384, 8192], P('dp', 'tensor'), may hold values from -6 to 6
- ref_gain: float32 [8192], P('tensor'), may hold values from 0.1 to 1.9
- ref_weight: bfloat16 [8192, 512], P('tensor'), may hold values from -0.0625 to 0.0625
- pol_gain: float32 [8192], replicated, may hold values from 0.1 to 1.9
- pol_weight: bfloat16 [8192, 512], P('dp'), may hold values from -0.0625 to 0.0625
- lengths: int32 [16, 8, 16], P('dp', 'tensor'), may hold values from 1 to 16, 128 in all within a row
- bins: int32 [16, 8, 16], P('dp', 'tensor'), may hold values from 0 to 15, each once within a row
- advantage: float32 [16, 8, 16], P('dp', 'tensor'), may hold values from -4 to 4
- logprob_gap: float32 [16384], P(('dp', 'tensor')), may hold values from -1 to 1
- cotangent: bfloat16 [16, 8, 256, 512], P('dp', 'tensor'), may hold values from -6 to 6
Outputs:
- policy_values: bfloat16 [16, 8, 256, 512], P('dp', 'tensor')
- grad_weight: float32 [8192, 512], P(('dp', 'tensor'))
Inputs may be any that keep to these rules, and one draw needn't show every extreme that they name: `lengths`: lengths of the 16 sequences of one run, in the order in which they lie in it; they sum to 128, and the longest of every run is exactly 16. The sequences of one run go to distinct bins: each bin takes exactly one sequence of every run.
All inputs are finite; a program needn't handle non-finite values.
Results may differ from a plain program's by a relative error of at most 0.015.
Values may be sent and summed in bfloat16 or wider, within the bound.
A program may use at most 64 MiB of HBM per device.

v0:
```python
import math
import jax
import jax.numpy as jnp
from jax import lax
from jax.sharding import PartitionSpec as P

EPS = 1e-06
BETA = 1.0


def rounded(values):
    return lax.optimization_barrier(values.astype(jnp.bfloat16)).astype(jnp.float32)


def on_device(
    tokens,
    ref_gain,
    ref_weight,
    pol_gain,
    pol_weight,
    lengths,
    bins,
    advantage,
    logprob_gap,
    cotangent,
):
    tensor_count = lax.axis_size("tensor")
    dp_count = lax.axis_size("dp")
    group_rows = tokens.shape[0]
    own_rows = group_rows // tensor_count
    slot_count = cotangent.shape[2]
    span_rows = slot_count // dp_count
    model_width = pol_gain.shape[0]
    value_width = ref_weight.shape[1]
    scaled = (tokens.astype(jnp.float32) * ref_gain[None, :]).astype(jnp.bfloat16)
    partial_value = rounded(jnp.dot(scaled, ref_weight, preferred_element_type=jnp.float32))
    summed = lax.psum(partial_value.astype(jnp.bfloat16), "tensor").astype(jnp.float32)
    owned_sum = lax.dynamic_slice_in_dim(summed, lax.axis_index("tensor") * own_rows, own_rows, 0)
    full_rows = lax.all_to_all(tokens, "tensor", split_axis=0, concat_axis=1, tiled=True)
    row_power = jnp.mean(jnp.square(full_rows.astype(jnp.float32)), axis=1)
    ref_values = (owned_sum * lax.rsqrt(row_power + EPS)[:, None]).astype(jnp.bfloat16)
    seq_lens = lengths.reshape(-1)
    seq_bins = bins.reshape(-1)
    seq_adv = advantage.reshape(-1)
    seq_starts = jnp.cumsum(seq_lens) - seq_lens
    chosen = seq_bins[None, :] == jnp.arange(dp_count, dtype=jnp.int32)[:, None]
    bin_len = jnp.sum(jnp.where(chosen, seq_lens[None, :], 0), axis=1)
    bin_start = jnp.sum(jnp.where(chosen, seq_starts[None, :], 0), axis=1)
    bin_adv = jnp.sum(jnp.where(chosen, seq_adv[None, :], jnp.float32(0.0)), axis=1)
    offsets = jnp.arange(span_rows, dtype=jnp.int32)
    usable = offsets[None, :] < bin_len[:, None]
    row_picks = jnp.clip(bin_start[:, None] + offsets[None, :], 0, own_rows - 1)
    send_rows = jnp.where(usable[:, :, None], full_rows[row_picks], jnp.zeros((), jnp.bfloat16))
    send_ref = jnp.where(usable[:, :, None], ref_values[row_picks], jnp.zeros((), jnp.bfloat16))
    len_float = bin_len.astype(jnp.float32)[:, None]
    importance = jnp.minimum(jnp.exp(logprob_gap[row_picks]), jnp.float32(2.0))
    coef_adv = jnp.where(
        usable, bin_adv[:, None] * importance / len_float, jnp.float32(0.0)
    ).astype(jnp.bfloat16)
    coef_pull = jnp.where(usable, BETA / len_float, jnp.float32(0.0)).astype(jnp.bfloat16)
    got_rows, got_ref, got_adv, got_pull = (
        lax.all_to_all(send_rows, "dp", split_axis=0, concat_axis=0, tiled=True),
        lax.all_to_all(send_ref, "dp", split_axis=0, concat_axis=0, tiled=True),
        lax.all_to_all(coef_adv, "dp", split_axis=0, concat_axis=0, tiled=True),
        lax.all_to_all(coef_pull, "dp", split_axis=0, concat_axis=0, tiled=True),
    )
    packed_rows = got_rows.reshape(slot_count, model_width)
    power = jnp.mean(jnp.square(packed_rows.astype(jnp.float32)), axis=1)
    normed = (
        packed_rows.astype(jnp.float32) * lax.rsqrt(power + EPS)[:, None] * pol_gain[None, :]
    ).astype(jnp.bfloat16)
    packed_ref = got_ref.reshape(slot_count, value_width).astype(jnp.float32)
    adv_column = got_adv.reshape(slot_count, 1).astype(jnp.float32)
    pull_column = got_pull.reshape(slot_count, 1).astype(jnp.float32)
    upstream = cotangent.reshape(slot_count, value_width).astype(jnp.float32)
    factor = 1.0 / math.sqrt(dp_count * tensor_count * seq_lens.shape[0])
    feature_block = normed
    values = jnp.dot(
        feature_block,
        lax.all_gather(pol_weight, "dp", axis=0, tiled=True),
        preferred_element_type=jnp.float32,
    )
    slope = (adv_column * upstream + pull_column * (values - packed_ref)).astype(jnp.bfloat16)
    feature_block = normed
    grad_weight = lax.psum_scatter(
        lax.dot_general(
            feature_block, slope, (((0,), (0,)), ((), ())), preferred_element_type=jnp.float32
        )
        * factor,
        ("dp", "tensor"),
        scatter_dimension=0,
        tiled=True,
    )
    policy_values = values.astype(jnp.bfloat16).reshape(1, 1, slot_count, value_width)
    return (policy_values, grad_weight)


def solution(mesh):
    in_specs = (
        P("dp", "tensor"),
        P("tensor"),
        P("tensor", None),
        P(),
        P("dp", None),
        P("dp", "tensor", None),
        P("dp", "tensor", None),
        P("dp", "tensor", None),
        P(("dp", "tensor")),
        P("dp", "tensor", None, None),
    )
    out_specs = (P("dp", "tensor", None, None), P(("dp", "tensor"), None))
    return jax.shard_map(
        on_device, mesh=mesh, in_specs=in_specs, out_specs=out_specs, check_vma=False
    )
```

profile of v0, /device:TPU:0, one launch (start us, length us, event | category | flops | bytes accessed | tf_op | source)
XLA Modules:
  0.0 858.9 jit_solution(14189858339868962872)
XLA Ops:
  8.0 0.0 copy-start
  8.0 0.0 all-reduce.2.cloned.1.call-start
  8.1 1.2 copy-done
  9.2 3.8 fusion.4
  13.1 0.0 all-reduce.2.cloned.1.call-update
  13.1 0.0 all-gather.2.cloned.1.call-start
  13.1 0.5 all-gather.2.cloned.1.call-update
  13.7 5.9 all-to-all-start
  19.6 0.1 copy.19
  19.7 0.1 reduce.2
  19.9 0.1 select_reduce_fusion.2
  20.0 0.1 compare_select_fusion
  20.0 0.1 reshape.312
  20.2 0.0 copy-start.8
  20.2 1.9 gather_fusion.1
  22.1 0.1 min.28
  22.2 0.1 select_reduce_fusion
  22.3 0.7 fusion.12
  23.0 0.7 fusion.13
  23.7 27.8 %all-to-all-done = bf16[8,128,1024]{2,1,0:T(8,128)(2,1)S(1)} async-done(((bf16[8,128,1024]{2,1,0:T(8,128)(2,1)}), bf16[8,128,1024]{2,1,0:T(8,128)(2,1)S(1)}, u32[]{:S(2)}, u32[]{:S(2)}) %all-to-all-start) | async-done | bytes 2097184 | tf_op jit(solution)/shard_map/all_to_all | solution.py:39
  51.5 7.6 all-to-all-start.2
  59.1 0.1 iota_compare_fusion.1
  59.2 1.8 copy.20
  61.0 5.2 gather_fusion
  66.2 0.4 all-to-all-done.2
  66.6 6.8 all-to-all-start.3
  73.4 4.5 broadcast_select_fusion
  77.9 3.0 all-to-all-done.3
  80.9 4.5 all-to-all-start.1
  85.5 0.1 reshape.306
  85.6 0.1 reshape.308
  85.7 0.5 multiply_reduce_fusion.1
  86.2 29.8 %all-reduce.2.cloned.1.call-done = bf16[1024,512]{1,0:T(8,128)(2,1)} async-done(((bf16[1024,512]{1,0:T(8,128)(2,1)}), bf16[1024,512]{1,0:T(8,128)(2,1)}) %all-reduce.2.cloned.1.call-update) | async-done | bytes 1048592 | tf_op jit(solution)/shard_map/psum | solution.py:37
  116.1 1.0 multiply_convert_fusion.4
  117.1 1.2 gather_fusion.2
  118.2 0.8 broadcast_select_fusion.1
  119.0 32.7 %all-to-all-done.1 = bf16[16,16,8192]{2,1,0:T(8,128)(2,1)} async-done(((bf16[16,16,8192]{2,1,0:T(8,128)(2,1)}), bf16[16,16,8192]{2,1,0:T(8,128)(2,1)}, u32[]{:S(2)}, u32[]{:S(2)}) %all-to-all-start.1) | async-done | bytes 4194336 | tf_op jit(solution)/shard_map/all_to_all | solution.py:62
  151.7 4.4 all-to-all-start.4
  156.1 0.2 reduce-scatter.2.cloned.1.call-start
  156.3 3.2 multiply_reduce_fusion
  159.6 0.1 rsqrt.18
  159.7 5.3 fusion.1
  165.0 7.0 fusion.14
  172.1 0.0 all-to-all-done.4
  172.1 10.4 %convolution_multiply_fusion = f32[8192,512]{1,0:T(8,128)} fusion(bf16[256,8192]{1,0:T(8,128)(2,1)} %fusion.1, f32[256,512]{1,0:T(8,128)S(1)} %fusion.14, bf16[256,512]{1,0:T(8,128)(2,1)S(1)} %bitcast.38, bf16[1,1,256,512]{3,2,1,0:T(8,128)(2,1)S(1)} %copy-done.4, f32[256]{0:T(256)S(1)} %reshape.308, f32[256]{0:T(256)S(1)} %reshape.306), kind=kOutput, calls=%fused_computation.3 | convolution fusion | flops 2152595456 | bytes 22022144 | tf_op jit(solution)/shard_map/dot_general | solution.py:86
  182.5 0.0 reduce-scatter.2.cloned.1.call-update
  182.5 0.7 convert_bitcast_fusion
  183.2 668.2 %reduce-scatter.2.cloned.1.call-done = f32[64,512]{1,0:T(8,128)} async-done(((f32[8192,512]{1,0:T(8,128)}), f32[64,512]{1,0:T(8,128)}) %reduce-scatter.2.cloned.1.call-update) | async-done | bytes 131088 | tf_op jit(solution)/shard_map/reduce_scatter | solution.py:85
  (26 shorter events, 0.2 us)
Async XLA Ops:
  8.0 1.2 copy-start
  8.0 108.1 %all-reduce.2.cloned.1.call-start = ((), (), s32[]{:S(2)}) async-start(), calls=%async_computation.7 | async-start | bytes 2097152 | tf_op jit(solution)/shard_map/psum | solution.py:37
  13.1 6.5 copy-start.6
  13.1 6.8 copy-start.7
  13.1 7.1 copy-start.1
  13.1 151.9 %all-gather.2.cloned.1.call-start = ((), (), s32[]{:S(2)}) async-start(), calls=%async_computation.6 | async-start | bytes 8912896 | tf_op jit(solution)/shard_map/all_gather | solution.py:80
  13.7 37.9 %all-to-all-start = ((bf16[8,128,1024]{2,1,0:T(8,128)(2,1)}), bf16[8,128,1024]{2,1,0:T(8,128)(2,1)S(1)}, u32[]{:S(2)}, u32[]{:S(2)}) async-start(bf16[8,128,1024]{2,1,0:T(8,128)(2,1)} %bitcast.37), calls=%async_computation | async-start | bytes 4194304 | tf_op jit(solution)/shard_map/all_to_all | solution.py:39
  20.2 2.0 copy-start.8
  51.5 7.7 copy-start.2
  51.5 15.1 %all-to-all-start.2 = ((bf16[16,1,16]{2,1,0:T(2,128)(2,1)}), bf16[16,1,16]{2,1,0:T(2,128)(2,1)S(1)}, u32[]{:S(2)}, u32[]{:S(2)}) async-start(bf16[16,1,16]{2,1,0:T(2,128)(2,1)} %fusion.13), calls=%async_computation.2 | async-start | bytes 16384 | tf_op jit(solution)/shard_map/all_to_all | solution.py:64
  66.6 14.3 %all-to-all-start.3 = ((bf16[16,1,16]{2,1,0:T(2,128)(2,1)}), bf16[16,1,16]{2,1,0:T(2,128)(2,1)S(1)}, u32[]{:S(2)}, u32[]{:S(2)}) async-start(bf16[16,1,16]{2,1,0:T(2,128)(2,1)} %fusion.12), calls=%async_computation.3 | async-start | bytes 16384 | tf_op jit(solution)/shard_map/all_to_all | solution.py:65
  77.9 7.8 copy-start.3
  80.9 70.8 %all-to-all-start.1 = ((bf16[16,16,8192]{2,1,0:T(8,128)(2,1)}), bf16[16,16,8192]{2,1,0:T(8,128)(2,1)}, u32[]{:S(2)}, u32[]{:S(2)}) async-start(bf16[16,16,8192]{2,1,0:T(8,128)(2,1)} %broadcast_select_fusion), calls=%async_computation.1 | async-start | bytes 8388608 | tf_op jit(solution)/shard_map/all_to_all | solution.py:62
  86.2 73.5 %copy-start.5 = (f32[8192]{0:T(1024)S(1)}, f32[8192]{0:T(1024)}, u32[]{:S(2)}) copy-start(f32[8192]{0:T(1024)} %param.13) | copy-start | bytes 98308
  151.7 20.3 %all-to-all-start.4 = ((bf16[16,16,512]{2,1,0:T(8,128)(2,1)}), bf16[16,16,512]{2,1,0:T(8,128)(2,1)S(1)}, u32[]{:S(2)}, u32[]{:S(2)}) async-start(bf16[16,16,512]{2,1,0:T(8,128)(2,1)} %broadcast_select_fusion.1), calls=%async_computation.4 | async-start | bytes 524288 | tf_op jit(solution)/shard_map/all_to_all | solution.py:63
  156.1 695.3 %reduce-scatter.2.cloned.1.call-start = ((), (), s32[]{:S(2)}) async-start(), calls=%async_computation.8 | async-start | bytes 16908288 | tf_op jit(solution)/shard_map/reduce_scatter | solution.py:85
  165.0 7.0 copy-start.4
Sparse Core Ops, SparseCore 0:
  13.2 102.8 all-reduce.1
  182.6 668.7 reduce-scatter.1
Sparse Core Ops, SparseCore 1:
  16.0 145.2 all-gather.1
where the time goes:
time: 860 us; the launch traced here: 859 us
  waiting for transfers between devices  763 us (89%)
  starting transfers between devices  29.6 us (3%)
  matrix products  21.2 us (2%)
  other arithmetic  18.1 us (2%)
  between operations  15.7 us (2%)
  local copies, waits for them, and re-layouts  11.7 us (1%)
    reduce_scatter x1, waiting for transfers between devices, on_device(): lax.psum_scatter(lax.dot_general(feature_block, slope, (((0,), (0,)), (()...  668 us
    all_to_all x1, waiting for transfers between devices, on_device(): lax.all_to_all(send_rows, 'dp', split_axis=0, concat_axis=0, tiled=True)  32.7 us
    psum x1, waiting for transfers between devices, on_device(): lax.psum(partial_value.astype(jnp.bfloat16), 'tensor').astype(jnp.float32)  29.8 us
    all_to_all x1, waiting for transfers between devices, on_device(): lax.all_to_all(tokens, 'tensor', split_axis=0, concat_axis=1, tiled=True)  27.8 us
  transfers between devices with their start and end apart: 8, of which 6 were waited for; matrix products, arithmetic and copies ran while one was open for 4% of the time, Pallas kernels for 0%

commit v1 on v0

--- a/solution.py
+++ b/solution.py
@@ -36,7 +36,12 @@
     partial_value = rounded(jnp.dot(scaled, ref_weight, preferred_element_type=jnp.float32))
     summed = lax.psum(partial_value.astype(jnp.bfloat16), "tensor").astype(jnp.float32)
     owned_sum = lax.dynamic_slice_in_dim(summed, lax.axis_index("tensor") * own_rows, own_rows, 0)
-    full_rows = lax.all_to_all(tokens, "tensor", split_axis=0, concat_axis=1, tiled=True)
+    full_rows = jnp.concatenate(
+        lax.all_to_all(
+            jnp.stack(jnp.split(tokens, lax.axis_size("tensor"), axis=0)), "tensor", 0, 0
+        ),
+        axis=1,
+    )
     row_power = jnp.mean(jnp.square(full_rows.astype(jnp.float32)), axis=1)
     ref_values = (owned_sum * lax.rsqrt(row_power + EPS)[:, None]).astype(jnp.bfloat16)
     seq_lens = lengths.reshape(-1)

time: 860 us -> 868 us (level)
  transfers between devices with their start and end apart: 8 -> 8, of which waited for: 6 -> 6; matrix products, arithmetic and copies ran while one was open for 4% -> 5% of each run, Pallas kernels for 0% -> 0%
where the time goes in v1:
time: 868 us
  waiting for transfers between devices  761 us (88%)
  starting transfers between devices  34.2 us (4%)
  matrix products  21.2 us (2%)
  other arithmetic  18 us (2%)
  local copies, waits for them, and re-layouts  17.6 us (2%)
  between operations  15.7 us (2%)
    reduce_scatter x1, waiting for transfers between devices, on_device(): lax.psum_scatter(lax.dot_general(feature_block, slope, (((0,), (0,)), (()...  667 us
    all_to_all x1, waiting for transfers between devices, on_device(): lax.all_to_all(send_rows, 'dp', split_axis=0, concat_axis=0, tiled=True)  34.8 us
    all_to_all x1, waiting for transfers between devices, on_device(): lax.all_to_all(jnp.stack(jnp.split(tokens, lax.axis_size('tensor'), axis=...  31.1 us
    psum x1, waiting for transfers between devices, on_device(): lax.psum(partial_value.astype(jnp.bfloat16), 'tensor').astype(jnp.float32)  23.8 us
  transfers between devices with their start and end apart: 8, of which 6 were waited for; matrix products, arithmetic and copies ran while one was open for 5% of the time, Pallas kernels for 0%

profile of v1, /device:TPU:0, one launch (start us, length us, event | category | flops | bytes accessed | tf_op | source)
XLA Modules:
  0.0 867.6 jit_solution(14260503860598000691)
XLA Ops:
  8.1 1.2 copy-done
  9.2 3.8 fusion.4
  13.1 0.5 all-gather.2.cloned.1.call-update
  13.7 0.7 bitcast_dynamic-update-slice_fusion.7
  14.4 0.7 bitcast_dynamic-update-slice_fusion.6
  15.1 0.7 bitcast_dynamic-update-slice_fusion.5
  15.9 0.7 bitcast_dynamic-update-slice_fusion.4
  16.6 0.7 bitcast_dynamic-update-slice_fusion.3
  17.3 0.7 bitcast_dynamic-update-slice_fusion.2
  18.1 0.7 bitcast_dynamic-update-slice_fusion.1
  18.8 0.7 bitcast_dynamic-update-slice_fusion
  19.5 6.0 all-to-all-start
  25.6 0.1 copy.17
  25.7 0.1 reduce.2
  25.8 0.1 select_reduce_fusion.2
  25.9 0.1 compare_select_fusion
  26.0 0.1 reshape.317
  26.1 1.9 gather_fusion.1
  28.0 0.1 min.28
  28.1 0.1 select_reduce_fusion
  28.3 0.7 fusion.12
  29.0 0.7 fusion.13
  29.7 31.1 %all-to-all-done = bf16[8,128,1024]{2,1,0:T(8,128)(2,1)S(1)} async-done(((bf16[8,128,1024]{2,1,0:T(8,128)(2,1)}), bf16[8,128,1024]{2,1,0:T(8,128)(2,1)S(1)}, u32[]{:S(2)}, u32[]{:S(2)}) %all-to-all-start) | async-done | bytes 2097184 | tf_op jit(solution)/shard_map/all_to_all | solution.py:40
  60.8 7.5 all-to-all-start.2
  68.3 1.8 copy.18
  70.2 5.2 gather_fusion
  75.3 0.4 all-to-all-done.2
  75.7 6.8 all-to-all-start.3
  82.6 4.6 broadcast_select_fusion
  87.1 2.9 all-to-all-done.3
  90.0 4.6 all-to-all-start.1
  94.7 0.1 reshape.311
  94.8 0.1 reshape.313
  94.9 0.5 multiply_reduce_fusion.1
  95.4 23.8 %all-reduce.2.cloned.1.call-done = bf16[1024,512]{1,0:T(8,128)(2,1)} async-done(((bf16[1024,512]{1,0:T(8,128)(2,1)}), bf16[1024,512]{1,0:T(8,128)(2,1)}) %all-reduce.2.cloned.1.call-update) | async-done | bytes 1048592 | tf_op jit(solution)/shard_map/psum | solution.py:37
  119.1 1.0 multiply_convert_fusion.4
  120.1 1.2 gather_fusion.2
  121.3 0.8 broadcast_select_fusion.1
  122.1 34.8 %all-to-all-done.1 = bf16[16,16,8192]{2,1,0:T(8,128)(2,1)} async-done(((bf16[16,16,8192]{2,1,0:T(8,128)(2,1)}), bf16[16,16,8192]{2,1,0:T(8,128)(2,1)}, u32[]{:S(2)}, u32[]{:S(2)}) %all-to-all-start.1) | async-done | bytes 4194336 | tf_op jit(solution)/shard_map/all_to_all | solution.py:67
  156.9 9.0 %all-to-all-start.4 = ((bf16[16,16,512]{2,1,0:T(8,128)(2,1)}), bf16[16,16,512]{2,1,0:T(8,128)(2,1)S(1)}, u32[]{:S(2)}, u32[]{:S(2)}) async-start(bf16[16,16,512]{2,1,0:T(8,128)(2,1)} %broadcast_select_fusion.1), calls=%async_computation.4 | async-start | bytes 524288 | tf_op jit(solution)/shard_map/all_to_all | solution.py:68
  166.0 0.2 reduce-scatter.2.cloned.1.call-start
  166.2 3.1 multiply_reduce_fusion
  169.3 0.1 rsqrt.18
  169.4 5.3 fusion.1
  174.7 7.0 fusion.14
  181.7 10.4 %convolution_multiply_fusion = f32[8192,512]{1,0:T(8,128)} fusion(bf16[256,8192]{1,0:T(8,128)(2,1)} %fusion.1, f32[256,512]{1,0:T(8,128)S(1)} %fusion.14, bf16[256,512]{1,0:T(8,128)(2,1)S(1)} %bitcast.52, bf16[1,1,256,512]{3,2,1,0:T(8,128)(2,1)S(1)} %copy-done.5, f32[256]{0:T(256)S(1)} %reshape.313, f32[256]{0:T(256)S(1)} %reshape.311), kind=kOutput, calls=%fused_computation.3 | convolution fusion | flops 2152595456 | bytes 22022144 | tf_op jit(solution)/shard_map/dot_general | solution.py:91
  192.1 0.7 convert_bitcast_fusion
  192.9 667.3 %reduce-scatter.2.cloned.1.call-done = f32[64,512]{1,0:T(8,128)} async-done(((f32[8192,512]{1,0:T(8,128)}), f32[64,512]{1,0:T(8,128)}) %reduce-scatter.2.cloned.1.call-update) | async-done | bytes 131088 | tf_op jit(solution)/shard_map/reduce_scatter | solution.py:90
  (36 shorter events, 0.4 us)
Async XLA Ops:
  8.0 1.2 copy-start
  8.0 5.7 copy-start.4
  8.0 111.1 %all-reduce.2.cloned.1.call-start = ((), (), s32[]{:S(2)}) async-start(), calls=%async_computation.7 | async-start | bytes 2097152 | tf_op jit(solution)/shard_map/psum | solution.py:37
  13.1 161.6 %all-gather.2.cloned.1.call-start = ((), (), s32[]{:S(2)}) async-start(), calls=%async_computation.6 | async-start | bytes 8912896 | tf_op jit(solution)/shard_map/all_gather | solution.py:85
  19.5 6.0 copy-start.7
  19.5 6.3 copy-start.8
  19.5 6.6 copy-start.1
  19.5 41.2 %all-to-all-start = ((bf16[8,128,1024]{2,1,0:T(8,128)(2,1)}), bf16[8,128,1024]{2,1,0:T(8,128)(2,1)S(1)}, u32[]{:S(2)}, u32[]{:S(2)}) async-start(bf16[8,128,1024]{2,1,0:T(8,128)(2,1)} %bitcast_dynamic-update-slice_fusion), calls=%async_computation | async-start | bytes 4194304 | tf_op jit(solution)/shard_map/all_to_all | solution.py:40
  26.1 2.0 copy-start.9
  60.8 7.6 copy-start.2
  60.8 15.0 %all-to-all-start.2 = ((bf16[16,1,16]{2,1,0:T(2,128)(2,1)}), bf16[16,1,16]{2,1,0:T(2,128)(2,1)S(1)}, u32[]{:S(2)}, u32[]{:S(2)}) async-start(bf16[16,1,16]{2,1,0:T(2,128)(2,1)} %fusion.13), calls=%async_computation.2 | async-start | bytes 16384 | tf_op jit(solution)/shard_map/all_to_all | solution.py:69
  75.7 14.3 %all-to-all-start.3 = ((bf16[16,1,16]{2,1,0:T(2,128)(2,1)}), bf16[16,1,16]{2,1,0:T(2,128)(2,1)S(1)}, u32[]{:S(2)}, u32[]{:S(2)}) async-start(bf16[16,1,16]{2,1,0:T(2,128)(2,1)} %fusion.12), calls=%async_computation.3 | async-start | bytes 16384 | tf_op jit(solution)/shard_map/all_to_all | solution.py:70
  87.1 7.8 copy-start.3
  90.0 66.9 %all-to-all-start.1 = ((bf16[16,16,8192]{2,1,0:T(8,128)(2,1)}), bf16[16,16,8192]{2,1,0:T(8,128)(2,1)}, u32[]{:S(2)}, u32[]{:S(2)}) async-start(bf16[16,16,8192]{2,1,0:T(8,128)(2,1)} %broadcast_select_fusion), calls=%async_computation.1 | async-start | bytes 8388608 | tf_op jit(solution)/shard_map/all_to_all | solution.py:67
  156.9 24.8 %all-to-all-start.4 = ((bf16[16,16,512]{2,1,0:T(8,128)(2,1)}), bf16[16,16,512]{2,1,0:T(8,128)(2,1)S(1)}, u32[]{:S(2)}, u32[]{:S(2)}) async-start(bf16[16,16,512]{2,1,0:T(8,128)(2,1)} %broadcast_select_fusion.1), calls=%async_computation.4 | async-start | bytes 524288 | tf_op jit(solution)/shard_map/all_to_all | solution.py:68
  166.0 3.4 copy-start.6
  166.0 694.2 %reduce-scatter.2.cloned.1.call-start = ((), (), s32[]{:S(2)}) async-start(), calls=%async_computation.8 | async-start | bytes 16908288 | tf_op jit(solution)/shard_map/reduce_scatter | solution.py:90
  174.7 7.0 copy-start.5
Sparse Core Ops, SparseCore 0:
  13.2 105.8 all-reduce.1
  192.3 667.8 reduce-scatter.1
Sparse Core Ops, SparseCore 1:
  16.0 147.6 all-gather.1
